TPU v7x, 256 devices: a whole 4x4x8 slice. The times are simulated.
256 devices in a mesh: expert: 64 (over y, x, z_lo), dp: 4 (over z_hi, core).
Axes of the slice: x: 4, y: 4, z: 8 (z_hi: 2, z_lo: 4; z = z_hi * 4 + z_lo), core: 2. Of those that a mesh axis runs over, the one named last changes fastest.
Arguments:
- tokens: bfloat16 [3072, 3584], P('expert'), may hold values from -6 to 6
- expert_weights: bfloat16 [64, 3, 3584, 1024], P('expert', None, None, 'dp'), may hold values from -0.09375 to 0.09375
- partner: int32 [64], replicated, may hold values from 0 to 63, as said below
- replica: int32 [64], replicated, may hold values from 0 to 63, as said below
- routing: int32 [3072, 8], P('expert'), may hold values from 0 to 127, all different within a row; in each aligned block of 48 rows (0 to 47, 48 to 95, ...) at most 6 rows name the same one
- gates: bfloat16 [3072, 8], P('expert'), may hold values from 0.099609375 to 1
Outputs:
- mixed: bfloat16 [3072, 3584], P('expert', 'dp')
Inputs may be any that keep to these rules, and one draw needn't show every extreme that they name: partner pairs devices: partner[partner[p]] = p; about half of the indices are paired with another, the rest with themselves. No expert appears more than 4 times in replica, and some expert appears exactly 4 times. `routing`: each row names 8 different slots; among the 48 rows of one device along expert no slot is named more than 6 times.
All inputs are finite; a program needn't handle non-finite values.
Results may differ from a plain program's by a relative error of at most 0.0058.
Values may be sent and summed in bfloat16 or wider, within the bound.
A program may use at most 128 MiB of HBM per device.

v0:
```python
import jax
import jax.numpy as jnp
from jax import lax
from jax.sharding import PartitionSpec as P


def dispatch(targets, group_count, group_depth, tokens, gates):
    tok_rows, choose_count = targets.shape
    pair_count = tok_rows * choose_count
    onehot = (
        targets.reshape(-1)[:, None] == jnp.arange(group_count, dtype=jnp.int32)[None, :]
    ).astype(jnp.float32)
    earlier_mask = (jnp.arange(pair_count)[:, None] > jnp.arange(pair_count)[None, :]).astype(
        jnp.float32
    )
    earlier = jnp.dot(earlier_mask, onehot, precision=lax.Precision.HIGHEST)
    position = jnp.sum(earlier * onehot, axis=1)
    position_hit = (
        position[:, None] == jnp.arange(group_depth, dtype=jnp.float32)[None, :]
    ).astype(jnp.float32)
    placed = (onehot[:, :, None] * position_hit[:, None, :]).reshape(
        tok_rows, choose_count, group_count * group_depth
    )
    spread = jnp.sum(placed, axis=1).astype(jnp.bfloat16)
    combine_weights = jnp.sum(placed * gates.astype(jnp.float32)[:, :, None], axis=1).astype(
        jnp.bfloat16
    )
    outgoing = jnp.einsum("tg,td->gd", spread, tokens, preferred_element_type=jnp.float32).astype(
        jnp.bfloat16
    )
    return (outgoing, combine_weights)


def shards(tokens, expert_weights, partner, replica, routing, gates):
    tok_rows, features = tokens.shape
    choose_count = routing.shape[1]
    expert_count = lax.axis_size("expert")
    slot_count = 2 * expert_count
    capacity = max(2, 2 * tok_rows * choose_count // slot_count)
    slot_table = jnp.stack([partner, replica], axis=1)
    outgoing, combine_weights = dispatch(routing, slot_count, capacity, tokens, gates)
    pieces = lax.all_to_all(expert_weights, "expert", split_axis=2, concat_axis=0, tiled=True)
    chosen = jnp.take(pieces, slot_table, axis=0)
    slot_weights = lax.all_to_all(chosen, "expert", split_axis=0, concat_axis=0, tiled=True)
    arrived = lax.all_to_all(
        outgoing.reshape(expert_count, 2, capacity, features),
        "expert",
        split_axis=0,
        concat_axis=0,
        tiled=True,
    )
    arrived_split = arrived.reshape(
        expert_count, 2, capacity, expert_count, features // expert_count
    )
    gate_up = jnp.einsum(
        "njcmd,mjwdf->wjncf",
        arrived_split,
        slot_weights[:, :, 0:2],
        preferred_element_type=jnp.float32,
    )
    hidden = (jax.nn.silu(gate_up[0]) * gate_up[1]).astype(jnp.bfloat16)
    down_rows = jnp.einsum(
        "jncf,mjdf->njcmd", hidden, slot_weights[:, :, 2], preferred_element_type=jnp.float32
    ).astype(jnp.bfloat16)
    returned = lax.all_to_all(
        down_rows.reshape(expert_count, 2, capacity, features),
        "expert",
        split_axis=0,
        concat_axis=0,
        tiled=True,
    )
    flat_back = returned.reshape(-1, features)
    partial_value = jnp.dot(combine_weights, flat_back, preferred_element_type=jnp.float32)
    return lax.psum_scatter(partial_value, "dp", scatter_dimension=1, tiled=True).astype(
        jnp.bfloat16
    )


def solution(mesh):
    return jax.shard_map(
        shards,
        mesh=mesh,
        in_specs=(
            P("expert", None),
            P("expert", None, None, "dp"),
            P(),
            P(),
            P("expert", None),
            P("expert", None),
        ),
        out_specs=P("expert", "dp"),
        check_vma=False,
    )
```

profile of v0, /device:TPU:1, one launch (start us, length us, event | category | flops | bytes accessed | tf_op | source)
XLA Modules:
  0.0 867.6 jit_solution(4485287671439022908)
XLA Ops:
  6.5 9.5 %copy.66 = bf16[1,3,3584,256]{3,1,0,2:T(4,128)(2,1)} copy(bf16[1,3,3584,256]{3,2,1,0:T(8,128)(2,1)} %param.7) | data formatting | bytes 11010048 | tf_op args[1]
  16.0 12.9 %all-to-all-start = ((bf16[1,3,3584,256]{3,1,0,2:T(4,128)(2,1)}), bf16[1,3,3584,256]{3,1,0,2:T(4,128)(2,1)}, u32[]{:S(2)}, u32[]{:S(2)}) async-start(bf16[1,3,3584,256]{3,1,0,2:T(4,128)(2,1)} %copy.66), calls=%async_computation | async-start | bytes 14680064 | tf_op jit(solution)/shard_map/all_to_all | solution.py:42
  29.5 12.1 %mul.39 = f32[48,8,768]{1,0,2:T(8,128)} reshape(f32[384,128,6]{0,2,1:T(8,128)S(1)} %broadcast_multiply_fusion) | data formatting | bytes 2359296 | tf_op jit(solution)/shard_map/mul | solution.py:21
  41.7 12.4 %multiply_reduce_fusion = (bf16[48,768]{0,1:T(8,128)(2,1)S(1)}, bf16[48,768]{0,1:T(8,128)(2,1)S(1)}) fusion(f32[48,8,768]{1,0,2:T(8,128)} %mul.39, f32[48,8]{1,0:T(8,128)S(1)} %copy.64), kind=kLoop, calls=%fused_computation.1 | loop fusion | flops 811008 | bytes 1328640 | tf_op jit(solution)/shard_map/reduce_sum | solution.py:25
  58.1 9.6 %reshape.157 = bf16[64,2,6,3584]{3,2,1,0:T(8,128)(2,1)} reshape(bf16[768,3584]{1,0:T(8,128)(2,1)} %convolution_convert_fusion) | data formatting | bytes 11010048 | tf_op jit(solution)/shard_map/reshape | solution.py:46
  67.6 9.4 %copy.72 = bf16[64,2,6,3584]{3,1,2,0:T(2,128)(2,1)} copy(bf16[64,2,6,3584]{3,2,1,0:T(8,128)(2,1)} %reshape.157) | data formatting | bytes 11010048 | tf_op jit(solution)/shard_map/reshape | solution.py:46
  77.0 114.0 %all-to-all-done = bf16[1,3,3584,256]{3,1,0,2:T(4,128)(2,1)} async-done(((bf16[1,3,3584,256]{3,1,0,2:T(4,128)(2,1)}), bf16[1,3,3584,256]{3,1,0,2:T(4,128)(2,1)}, u32[]{:S(2)}, u32[]{:S(2)}) %all-to-all-start) | async-done | bytes 5505056 | tf_op jit(solution)/shard_map/all_to_all | solution.py:42
  191.0 18.4 %all-to-all-start.2 = ((bf16[64,2,6,3584]{3,1,2,0:T(2,128)(2,1)}), bf16[64,2,6,3584]{3,1,2,0:T(2,128)(2,1)}, u32[]{:S(2)}, u32[]{:S(2)}) async-start(bf16[64,2,6,3584]{3,1,2,0:T(2,128)(2,1)} %copy.72), calls=%async_computation.2 | async-start | bytes 11010048 | tf_op jit(solution)/shard_map/all_to_all | solution.py:45
  209.9 6.6 copy.102
  216.5 10.5 %gather_fusion = bf16[128,3,56,256]{3,2,1,0:T(8,128)(2,1)} fusion(bf16[64,3,56,256]{3,2,1,0:T(8,128)(2,1)} %bitcast.71, s32[1024]{0:T(1024)S(1)} %pad_clamp_fusion), kind=kCustom, calls=%fused_computation | custom fusion | bytes 22020608 | tf_op jit(solution)/shard_map/jit(_take)/gather | solution.py:43
  227.0 10.3 %broadcast_select_fusion = bf16[64,2,3,56,256]{4,3,2,1,0:T(8,128)(2,1)} fusion(bf16[64,2,3,56,256]{4,3,2,1,0:T(8,128)(2,1)} %bitcast.72, pred[64,2]{1,0:T(8,128)(4,1)S(1)} %copy.65), kind=kLoop, calls=%fused_computation.3 | loop fusion | flops 5505024 | bytes 22020224 | tf_op jit(solution)/shard_map/jit(_take)/select_n | solution.py:43
  237.3 94.2 %all-to-all-done.2 = bf16[64,2,6,3584]{3,1,2,0:T(2,128)(2,1)} async-done(((bf16[64,2,6,3584]{3,1,2,0:T(2,128)(2,1)}), bf16[64,2,6,3584]{3,1,2,0:T(2,128)(2,1)}, u32[]{:S(2)}, u32[]{:S(2)}) %all-to-all-start.2) | async-done | bytes 5505056 | tf_op jit(solution)/shard_map/all_to_all | solution.py:45
  331.5 10.9 %all-to-all-start.1 = ((bf16[64,2,3,56,256]{4,3,2,1,0:T(8,128)(2,1)}), bf16[64,2,3,56,256]{4,3,2,1,0:T(8,128)(2,1)}, u32[]{:S(2)}, u32[]{:S(2)}) async-start(bf16[64,2,3,56,256]{4,3,2,1,0:T(8,128)(2,1)} %broadcast_select_fusion), calls=%async_computation.1 | async-start | bytes 22020096 | tf_op jit(solution)/shard_map/all_to_all | solution.py:44
  342.4 30.0 %reshape.175 = bf16[64,2,6,64,56]{4,3,1,2,0:T(8,128)(2,1)} reshape(bf16[64,2,6,3584]{3,1,2,0:T(2,128)(2,1)} %all-to-all-done.2) | data formatting | bytes 11010048 | tf_op jit(solution)/shard_map/reshape | solution.py:52
  372.4 16.9 %copy.80 = bf16[64,2,6,64,56,1]{3,0,4,2,5,1:T(8,128)(2,1)} copy(bf16[64,2,6,64,56,1]{4,3,1,2,0,5:T(8,128)(2,1)} %bitcast.70) | data formatting | bytes 11010048 | tf_op jit(solution)/shard_map/reshape | solution.py:52
  389.2 195.2 %all-to-all-done.1 = bf16[64,2,3,56,256]{4,3,2,1,0:T(8,128)(2,1)} async-done(((bf16[64,2,3,56,256]{4,3,2,1,0:T(8,128)(2,1)}), bf16[64,2,3,56,256]{4,3,2,1,0:T(8,128)(2,1)}, u32[]{:S(2)}, u32[]{:S(2)}) %all-to-all-start.1) | async-done | bytes 11010080 | tf_op jit(solution)/shard_map/all_to_all | solution.py:44
  584.5 7.5 slice.19
  593.3 8.7 fusion.1
  602.0 8.8 %convert_bitcast_fusion = bf16[64,2,6,64,56]{0,4,2,3,1:T(8,128)(2,1)} fusion(f32[2,2,64,6,256]{4,2,3,0,1:T(8,128)S(1)} %fusion.1, bf16[64,2,3,56,256]{4,3,2,1,0:T(8,128)(2,1)} %all-to-all-done.1), kind=kOutput, calls=%fused_computation.2 | convolution fusion | flops 1413218304 | bytes 10747904 | tf_op jit(solution)/shard_map/jncf,mjdf->njcmd/dot_general | solution.py:62
  610.8 17.3 %copy.90 = bf16[64,2,6,64,56]{4,3,1,2,0:T(8,128)(2,1)} copy(bf16[64,2,6,64,56]{0,4,2,3,1:T(8,128)(2,1)} %convert_bitcast_fusion) | data formatting | bytes 11010048 | tf_op jit(solution)/shard_map/reshape | solution.py:66
  628.1 28.5 %reshape.176 = bf16[64,2,6,3584]{3,1,2,0:T(2,128)(2,1)} reshape(bf16[64,2,6,64,56]{4,3,1,2,0:T(8,128)(2,1)} %copy.90) | data formatting | bytes 11010048 | tf_op jit(solution)/shard_map/reshape | solution.py:66
  656.6 144.7 %all_to_all.33 = bf16[64,2,6,3584]{3,1,2,0:T(2,128)(2,1)S(1)} all-to-all(bf16[64,2,6,3584]{3,1,2,0:T(2,128)(2,1)} %reshape.176), channel_id=1, replica_groups=mesh['expert'=64,'dp'=4] {'expert'}, dimensions={0} | all-to-all | bytes 11010048 | tf_op jit(solution)/shard_map/all_to_all | solution.py:65
  806.0 9.7 %reshape.160 = bf16[768,3584]{1,0:T(8,128)(2,1)} reshape(bf16[64,2,6,3584]{3,2,1,0:T(8,128)(2,1)} %copy.78) | data formatting | bytes 11010048 | tf_op jit(solution)/shard_map/reshape | solution.py:72
  820.2 39.0 %reduce-scatter.2.cloned.1.call-done = f32[48,896]{1,0:T(8,128)} async-done(((f32[48,3584]{1,0:T(8,128)}), f32[48,896]{1,0:T(8,128)}) %reduce-scatter.2.cloned.1.call-update) | async-done | bytes 172048 | tf_op jit(solution)/shard_map/reduce_scatter | solution.py:74
  (33 shorter events, 17.2 us)
Async XLA Ops:
  6.5 47.6 %copy-start = (bf16[48,3584]{1,0:T(8,128)(2,1)S(1)}, bf16[48,3584]{1,0:T(8,128)(2,1)}, u32[]{:S(2)}) copy-start(bf16[48,3584]{1,0:T(8,128)(2,1)} %param.6) | copy-start | bytes 1032196
  16.0 12.9 %copy-start.3 = (s32[48,8]{0,1:T(8,128)S(1)}, s32[48,8]{0,1:T(8,128)}, u32[]{:S(2)}) copy-start(s32[48,8]{0,1:T(8,128)} %param.10) | copy-start | bytes 4612
  16.0 175.0 %all-to-all-start = ((bf16[1,3,3584,256]{3,1,0,2:T(4,128)(2,1)}), bf16[1,3,3584,256]{3,1,0,2:T(4,128)(2,1)}, u32[]{:S(2)}, u32[]{:S(2)}) async-start(bf16[1,3,3584,256]{3,1,0,2:T(4,128)(2,1)} %copy.66), calls=%async_computation | async-start | bytes 14680064 | tf_op jit(solution)/shard_map/all_to_all | solution.py:42
  29.5 12.1 %copy-start.4 = (bf16[48,8]{0,1:T(8,128)(2,1)S(1)}, bf16[48,8]{0,1:T(8,128)(2,1)}, u32[]{:S(2)}) copy-start(bf16[48,8]{0,1:T(8,128)(2,1)} %param.11) | copy-start | bytes 2308
  77.0 132.4 %copy-start.5 = (s32[64]{0:T(128)S(1)}, s32[64]{0:T(128)}, u32[]{:S(2)}) copy-start(s32[64]{0:T(128)} %param.9) | copy-start | bytes 772
  77.0 132.4 %copy-start.6 = (s32[64]{0:T(128)S(1)}, s32[64]{0:T(128)}, u32[]{:S(2)}) copy-start(s32[64]{0:T(128)} %param.8) | copy-start | bytes 772
  191.0 140.5 %all-to-all-start.2 = ((bf16[64,2,6,3584]{3,1,2,0:T(2,128)(2,1)}), bf16[64,2,6,3584]{3,1,2,0:T(2,128)(2,1)}, u32[]{:S(2)}, u32[]{:S(2)}) async-start(bf16[64,2,6,3584]{3,1,2,0:T(2,128)(2,1)} %copy.72), calls=%async_computation.2 | async-start | bytes 11010048 | tf_op jit(solution)/shard_map/all_to_all | solution.py:45
  331.5 253.0 %all-to-all-start.1 = ((bf16[64,2,3,56,256]{4,3,2,1,0:T(8,128)(2,1)}), bf16[64,2,3,56,256]{4,3,2,1,0:T(8,128)(2,1)}, u32[]{:S(2)}, u32[]{:S(2)}) async-start(bf16[64,2,3,56,256]{4,3,2,1,0:T(8,128)(2,1)} %broadcast_select_fusion), calls=%async_computation.1 | async-start | bytes 22020096 | tf_op jit(solution)/shard_map/all_to_all | solution.py:44
  342.4 516.9 %reduce-scatter.2.cloned.1.call-start = ((), (), s32[]{:S(2)}) async-start(), calls=%async_computation.5 | async-start | bytes 860160 | tf_op jit(solution)/shard_map/reduce_scatter | solution.py:74
  584.5 8.9 %copy-start.2 = (bf16[64,2,6,64,56,1]{3,0,4,2,5,1:T(8,128)(2,1)S(1)}, bf16[64,2,6,64,56,1]{3,0,4,2,5,1:T(8,128)(2,1)}, u32[]{:S(2)}) copy-start(bf16[64,2,6,64,56,1]{3,0,4,2,5,1:T(8,128)(2,1)} %copy.80) | copy-start | bytes 16515076
  801.3 59.5 %copy-start.1 = (bf16[48,3584]{1,0:T(8,128)(2,1)S(1)}, bf16[48,3584]{1,0:T(8,128)(2,1)}, u32[]{:S(2)}) copy-start(bf16[48,3584]{1,0:T(8,128)(2,1)} %param.6) | copy-start | bytes 1032196
Sparse Core Ops, SparseCore 0:
  820.3 38.8 reduce-scatter.1
where the time goes:
time: 870 us; the launch traced here: 868 us
  waiting for transfers between devices  442 us (51%)
  local copies, waits for them, and re-layouts  174 us (20%)
  blocking collectives  145 us (17%)
  starting transfers between devices  42.3 us (5%)
  matrix products  26.1 us (3%)
  other arithmetic  24.4 us (3%)
  between operations  13.5 us (2%)
    all_to_all x1, waiting for transfers between devices, shards(): lax.all_to_all(chosen, 'expert', split_axis=0, concat_axis=0, tiled=True)  195 us
    all_to_all x1, blocking collectives, shards(): lax.all_to_all(down_rows.reshape(expert_count, 2, capacity, features), 'e...  145 us
    all_to_all x1, waiting for transfers between devices, shards(): lax.all_to_all(expert_weights, 'expert', split_axis=2, concat_axis=0, til...  114 us
    all_to_all x1, waiting for transfers between devices, shards(): lax.all_to_all(outgoing.reshape(expert_count, 2, capacity, features), 'ex...  94.2 us
    reshape x2, local copies, waits for them, and re-layouts, shards(): arrived.reshape(expert_count, 2, capacity, expert_count, features // expe...  46.8 us
    reshape x2, local copies, waits for them, and re-layouts, shards(): down_rows.reshape(expert_count, 2, capacity, features)  45.8 us
    reduce_scatter x1, waiting for transfers between devices, shards(): lax.psum_scatter(partial_value, 'dp', scatter_dimension=1, tiled=True)  39 us
    reshape x2, local copies, waits for them, and re-layouts, shards(): outgoing.reshape(expert_count, 2, capacity, features)  19 us
  transfers between devices with their start and end apart: 4, of which 4 were waited for; matrix products, arithmetic and copies ran while one was open for 14% of the time, Pallas kernels for 0%

commit v1 on v0

--- a/solution.py
+++ b/solution.py
@@ -39,7 +39,12 @@
     capacity = max(2, 2 * tok_rows * choose_count // slot_count)
     slot_table = jnp.stack([partner, replica], axis=1)
     outgoing, combine_weights = dispatch(routing, slot_count, capacity, tokens, gates)
-    pieces = lax.all_to_all(expert_weights, "expert", split_axis=2, concat_axis=0, tiled=True)
+    pieces = jnp.concatenate(
+        lax.all_to_all(
+            jnp.stack(jnp.split(expert_weights, lax.axis_size("expert"), axis=2)), "expert", 0, 0
+        ),
+        axis=0,
+    )
     chosen = jnp.take(pieces, slot_table, axis=0)
     slot_weights = lax.all_to_all(chosen, "expert", split_axis=0, concat_axis=0, tiled=True)
     arrived = lax.all_to_all(

time: 870 us -> 910 us (1.046)
  local copies, waits for them, and re-layouts: 174 us -> 256 us
  waiting for transfers between devices: 442 us -> 408 us
  starting transfers between devices: 42.3 us -> 31.6 us
    unnamed x16 -> x78, local copies, waits for them, and re-layouts: 11 us -> 97.8 us
    all_to_all x1, waiting for transfers between devices: 114 us -> 74.2 us  [shards(): lax.all_to_all(jnp.stack(jnp.split(expert_weights, lax.axis_size('expert'...]
  transfers between devices with their start and end apart: 4 -> 4, of which waited for: 4 -> 4; matrix products, arithmetic and copies ran while one was open for 14% -> 13% of each run, Pallas kernels for 0% -> 0%
where the time goes in v1:
time: 910 us; the launch traced here: 906 us
  waiting for transfers between devices  408 us (45%)
  local copies, waits for them, and re-layouts  256 us (28%)
  blocking collectives  146 us (16%)
  starting transfers between devices  31.6 us (3%)
  matrix products  26.1 us (3%)
  other arithmetic  24.4 us (3%)
  between operations  13.6 us (1%)
    all_to_all x1, waiting for transfers between devices, shards(): lax.all_to_all(chosen, 'expert', split_axis=0, concat_axis=0, tiled=True)  194 us
    all_to_all x1, blocking collectives, shards(): lax.all_to_all(down_rows.reshape(expert_count, 2, capacity, features), 'e...  146 us
    all_to_all x1, waiting for transfers between devices, shards(): lax.all_to_all(outgoing.reshape(expert_count, 2, capacity, features), 'ex...  102 us
    unnamed x78, local copies, waits for them, and re-layouts  97.8 us
    all_to_all x1, waiting for transfers between devices, shards(): lax.all_to_all(jnp.stack(jnp.split(expert_weights, lax.axis_size('expert'...  74.2 us
    reshape x2, local copies, waits for them, and re-layouts, shards(): arrived.reshape(expert_count, 2, capacity, expert_count, features // expe...  46.8 us
    reshape x2, local copies, waits for them, and re-layouts, shards(): down_rows.reshape(expert_count, 2, capacity, features)  45.8 us
    reduce_scatter x1, waiting for transfers between devices, shards(): lax.psum_scatter(partial_value, 'dp', scatter_dimension=1, tiled=True)  38.3 us
  transfers between devices with their start and end apart: 4, of which 4 were waited for; matrix products, arithmetic and copies ran while one was open for 13% of the time, Pallas kernels for 0%

profile of v1, /device:TPU:1, one launch (start us, length us, event | category | flops | bytes accessed | tf_op | source)
XLA Modules:
  0.0 906.0 jit_solution(9640002178113196414)
XLA Ops:
  104.3 12.9 %all-to-all-start = ((bf16[64,1,3,56,256]{4,3,2,1,0:T(8,128)(2,1)}), bf16[64,1,3,56,256]{4,3,2,1,0:T(8,128)(2,1)}, u32[]{:S(2)}, u32[]{:S(2)}) async-start(bf16[64,1,3,56,256]{4,3,2,1,0:T(8,128)(2,1)} %constant_dynamic-update-slice_fusion), calls=%async_computation | async-start | bytes 11010048 | tf_op jit(solution)/shard_map/all_to_all | solution.py:43
  117.9 12.1 %mul.39 = f32[48,8,768]{1,0,2:T(8,128)} reshape(f32[384,128,6]{0,2,1:T(8,128)S(1)} %broadcast_multiply_fusion) | data formatting | bytes 2359296 | tf_op jit(solution)/shard_map/mul | solution.py:21
  130.0 12.4 %multiply_reduce_fusion = (bf16[48,768]{0,1:T(8,128)(2,1)S(1)}, bf16[48,768]{0,1:T(8,128)(2,1)S(1)}) fusion(f32[48,8,768]{1,0,2:T(8,128)} %mul.39, f32[48,8]{1,0:T(8,128)S(1)} %copy.35), kind=kLoop, calls=%fused_computation.1 | loop fusion | flops 811008 | bytes 1328640 | tf_op jit(solution)/shard_map/reduce_sum | solution.py:25
  146.4 9.6 %reshape.161 = bf16[64,2,6,3584]{3,2,1,0:T(8,128)(2,1)} reshape(bf16[768,3584]{1,0:T(8,128)(2,1)} %convolution_convert_fusion) | data formatting | bytes 11010048 | tf_op jit(solution)/shard_map/reshape | solution.py:51
  156.0 9.4 %copy.40 = bf16[64,2,6,3584]{3,1,2,0:T(2,128)(2,1)} copy(bf16[64,2,6,3584]{3,2,1,0:T(8,128)(2,1)} %reshape.161) | data formatting | bytes 11010048 | tf_op jit(solution)/shard_map/reshape | solution.py:51
  165.4 74.2 %all-to-all-done = bf16[64,1,3,56,256]{4,3,2,1,0:T(8,128)(2,1)} async-done(((bf16[64,1,3,56,256]{4,3,2,1,0:T(8,128)(2,1)}), bf16[64,1,3,56,256]{4,3,2,1,0:T(8,128)(2,1)}, u32[]{:S(2)}, u32[]{:S(2)}) %all-to-all-start) | async-done | bytes 5505056 | tf_op jit(solution)/shard_map/all_to_all | solution.py:43
  239.6 10.1 %all-to-all-start.2 = ((bf16[64,2,6,3584]{3,1,2,0:T(2,128)(2,1)}), bf16[64,2,6,3584]{3,1,2,0:T(2,128)(2,1)}, u32[]{:S(2)}, u32[]{:S(2)}) async-start(bf16[64,2,6,3584]{3,1,2,0:T(2,128)(2,1)} %copy.40), calls=%async_computation.2 | async-start | bytes 11010048 | tf_op jit(solution)/shard_map/all_to_all | solution.py:50
  250.1 10.5 %gather_fusion = bf16[128,3,56,256]{3,2,1,0:T(8,128)(2,1)} fusion(bf16[64,3,56,256]{3,2,1,0:T(8,128)(2,1)} %bitcast.66, s32[1024]{0:T(1024)S(1)} %pad_clamp_fusion), kind=kCustom, calls=%fused_computation | custom fusion | bytes 22020608 | tf_op jit(solution)/shard_map/jit(_take)/gather | solution.py:48
  260.6 10.3 %broadcast_select_fusion = bf16[64,2,3,56,256]{4,3,2,1,0:T(8,128)(2,1)} fusion(bf16[64,2,3,56,256]{4,3,2,1,0:T(8,128)(2,1)} %bitcast.194, pred[64,2]{1,0:T(8,128)(4,1)S(1)} %copy.36), kind=kLoop, calls=%fused_computation.3 | loop fusion | flops 5505024 | bytes 22020224 | tf_op jit(solution)/shard_map/jit(_take)/select_n | solution.py:48
  270.9 101.7 %all-to-all-done.2 = bf16[64,2,6,3584]{3,1,2,0:T(2,128)(2,1)} async-done(((bf16[64,2,6,3584]{3,1,2,0:T(2,128)(2,1)}), bf16[64,2,6,3584]{3,1,2,0:T(2,128)(2,1)}, u32[]{:S(2)}, u32[]{:S(2)}) %all-to-all-start.2) | async-done | bytes 5505056 | tf_op jit(solution)/shard_map/all_to_all | solution.py:50
  372.6 8.6 all-to-all-start.1
  381.2 30.0 %reshape.179 = bf16[64,2,6,64,56]{4,3,1,2,0:T(8,128)(2,1)} reshape(bf16[64,2,6,3584]{3,1,2,0:T(2,128)(2,1)} %all-to-all-done.2) | data formatting | bytes 11010048 | tf_op jit(solution)/shard_map/reshape | solution.py:57
  411.2 16.9 %copy.48 = bf16[64,2,6,64,56,1]{3,0,4,2,5,1:T(8,128)(2,1)} copy(bf16[64,2,6,64,56,1]{4,3,1,2,0,5:T(8,128)(2,1)} %bitcast.193) | data formatting | bytes 11010048 | tf_op jit(solution)/shard_map/reshape | solution.py:57
  428.1 194.2 %all-to-all-done.1 = bf16[64,2,3,56,256]{4,3,2,1,0:T(8,128)(2,1)} async-done(((bf16[64,2,3,56,256]{4,3,2,1,0:T(8,128)(2,1)}), bf16[64,2,3,56,256]{4,3,2,1,0:T(8,128)(2,1)}, u32[]{:S(2)}, u32[]{:S(2)}) %all-to-all-start.1) | async-done | bytes 11010080 | tf_op jit(solution)/shard_map/all_to_all | solution.py:49
  622.2 7.5 slice.19
  631.1 8.7 fusion.1
  639.8 8.8 convert_bitcast_fusion
  648.6 17.3 %copy.56 = bf16[64,2,6,64,56]{4,3,1,2,0:T(8,128)(2,1)} copy(bf16[64,2,6,64,56]{0,4,2,3,1:T(8,128)(2,1)} %convert_bitcast_fusion) | data formatting | bytes 11010048 | tf_op jit(solution)/shard_map/reshape | solution.py:71
  665.9 28.5 %reshape.180 = bf16[64,2,6,3584]{3,1,2,0:T(2,128)(2,1)} reshape(bf16[64,2,6,64,56]{4,3,1,2,0:T(8,128)(2,1)} %copy.56) | data formatting | bytes 11010048 | tf_op jit(solution)/shard_map/reshape | solution.py:71
  694.4 146.0 %all_to_all.20 = bf16[64,2,6,3584]{3,1,2,0:T(2,128)(2,1)S(1)} all-to-all(bf16[64,2,6,3584]{3,1,2,0:T(2,128)(2,1)} %reshape.180), channel_id=1, replica_groups=mesh['expert'=64,'dp'=4] {'expert'}, dimensions={0} | all-to-all | bytes 11010048 | tf_op jit(solution)/shard_map/all_to_all | solution.py:70
  840.4 4.7 copy.46
  845.1 9.7 %reshape.164 = bf16[768,3584]{1,0:T(8,128)(2,1)} reshape(bf16[64,2,6,3584]{3,2,1,0:T(8,128)(2,1)} %copy.46) | data formatting | bytes 11010048 | tf_op jit(solution)/shard_map/reshape | solution.py:77
  854.8 4.5 fusion.14
  859.3 38.3 %reduce-scatter.2.cloned.1.call-done = f32[48,896]{1,0:T(8,128)} async-done(((f32[48,3584]{1,0:T(8,128)}), f32[48,896]{1,0:T(8,128)}) %reduce-scatter.2.cloned.1.call-update) | async-done | bytes 172048 | tf_op jit(solution)/shard_map/reduce_scatter | solution.py:79
  (95 shorter events, 105.8 us)
Async XLA Ops:
  6.5 135.9 %copy-start = (bf16[48,3584]{1,0:T(8,128)(2,1)S(1)}, bf16[48,3584]{1,0:T(8,128)(2,1)}, u32[]{:S(2)}) copy-start(bf16[48,3584]{1,0:T(8,128)(2,1)} %param.6) | copy-start | bytes 1032196
  104.3 12.9 %copy-start.3 = (s32[48,8]{0,1:T(8,128)S(1)}, s32[48,8]{0,1:T(8,128)}, u32[]{:S(2)}) copy-start(s32[48,8]{0,1:T(8,128)} %param.10) | copy-start | bytes 4612
  104.3 135.2 %all-to-all-start = ((bf16[64,1,3,56,256]{4,3,2,1,0:T(8,128)(2,1)}), bf16[64,1,3,56,256]{4,3,2,1,0:T(8,128)(2,1)}, u32[]{:S(2)}, u32[]{:S(2)}) async-start(bf16[64,1,3,56,256]{4,3,2,1,0:T(8,128)(2,1)} %constant_dynamic-update-slice_fusion), calls=%async_computation | async-start | bytes 11010048 | tf_op jit(solution)/shard_map/all_to_all | solution.py:43
  117.8 12.1 %copy-start.4 = (bf16[48,8]{0,1:T(8,128)(2,1)S(1)}, bf16[48,8]{0,1:T(8,128)(2,1)}, u32[]{:S(2)}) copy-start(bf16[48,8]{0,1:T(8,128)(2,1)} %param.11) | copy-start | bytes 2308
  165.4 84.3 %copy-start.5 = (s32[64]{0:T(128)S(1)}, s32[64]{0:T(128)}, u32[]{:S(2)}) copy-start(s32[64]{0:T(128)} %param.9) | copy-start | bytes 772
  165.4 84.3 %copy-start.6 = (s32[64]{0:T(128)S(1)}, s32[64]{0:T(128)}, u32[]{:S(2)}) copy-start(s32[64]{0:T(128)} %param.8) | copy-start | bytes 772
  239.6 133.0 %all-to-all-start.2 = ((bf16[64,2,6,3584]{3,1,2,0:T(2,128)(2,1)}), bf16[64,2,6,3584]{3,1,2,0:T(2,128)(2,1)}, u32[]{:S(2)}, u32[]{:S(2)}) async-start(bf16[64,2,6,3584]{3,1,2,0:T(2,128)(2,1)} %copy.40), calls=%async_computation.2 | async-start | bytes 11010048 | tf_op jit(solution)/shard_map/all_to_all | solution.py:50
  372.6 249.6 %all-to-all-start.1 = ((bf16[64,2,3,56,256]{4,3,2,1,0:T(8,128)(2,1)}), bf16[64,2,3,56,256]{4,3,2,1,0:T(8,128)(2,1)}, u32[]{:S(2)}, u32[]{:S(2)}) async-start(bf16[64,2,3,56,256]{4,3,2,1,0:T(8,128)(2,1)} %broadcast_select_fusion), calls=%async_computation.1 | async-start | bytes 22020096 | tf_op jit(solution)/shard_map/all_to_all | solution.py:49
  381.2 516.4 %reduce-scatter.2.cloned.1.call-start = ((), (), s32[]{:S(2)}) async-start(), calls=%async_computation.5 | async-start | bytes 860160 | tf_op jit(solution)/shard_map/reduce_scatter | solution.py:79
  622.2 8.9 copy-start.2
  845.1 54.1 %copy-start.1 = (bf16[48,3584]{1,0:T(8,128)(2,1)S(1)}, bf16[48,3584]{1,0:T(8,128)(2,1)}, u32[]{:S(2)}) copy-start(bf16[48,3584]{1,0:T(8,128)(2,1)} %param.6) | copy-start | bytes 1032196
Sparse Core Ops, SparseCore 0:
  859.4 38.1 reduce-scatter.1
